TPU v7x, 128 devices: a whole 4x4x4 slice. The times are simulated.
128 devices in a mesh: seq: 32 (over x, z, core), tp: 4 (over y).
Axes of the slice: x: 4, y: 4, z: 4, core: 2. Of those that a mesh axis runs over, the one named last changes fastest.
Arguments:
- hidden: bfloat16 [4096, 2560], P('seq'), may hold values from -6 to 6
- gain_attn: float32 [2560], replicated, may hold values from 0.5 to 1.5
- w_query: bfloat16 [2560, 2560], P(None, 'tp')
- w_key: bfloat16 [2560, 512], P(None, 'tp'), as said below
- w_value: bfloat16 [2560, 512], P(None, 'tp'), may hold values from -0.125 to 0.125
- w_out: bfloat16 [2560, 2560], P('tp'), may hold values from -0.125 to 0.125
- gain_moe: float32 [2560], replicated, may hold values from 0.5 to 1.5
- expert_ids: int32 [4096, 6], P('seq'), may hold values from 0 to 63, all different within a row; in each aligned block of 128 rows (0 to 127, 128 to 255, ...) at most 24 rows name the same one
- expert_gates: float32 [4096, 6], P('seq'), may hold values from 0.05 to 0.3
- w_gate: bfloat16 [64, 2560, 1536], P('seq', None, 'tp'), may hold values from -0.125 to 0.125
- w_up: bfloat16 [64, 2560, 1536], P('seq', None, 'tp'), may hold values from -0.125 to 0.125
- w_down: bfloat16 [64, 1536, 2560], P('seq', 'tp'), may hold values from -0.15625 to 0.15625
- seg_lengths: int32 [16], replicated, may hold values from 1 to 1024, 4096 in all
- slot_page: int32 [2048], replicated, may hold values from -1 to 255, as said below
Outputs:
- hidden_out: bfloat16 [4096, 2560], P('seq', 'tp')
- kv_cache: bfloat16 [2048, 16, 1024], P('seq', None, 'tp')
Inputs may be any that keep to these rules, and one draw needn't show every extreme that they name: `expert_ids`: a row names 6 different experts; within the 128 rows of one index of seq no expert is named by more than 24 rows. `seg_lengths`: segment lengths in order, summing to 4096. `slot_page`: owner o holds slots o * 64 to o * 64 + 63 as 2 requests of 32 slots; a request lists 1 to 32 consecutive pages (after the last page comes page 0), then -1 in its remaining slots. `w_key`: key projection of fan-in scale.
All inputs are finite; a program needn't handle non-finite values.
Results may differ from a plain program's by a relative error of at most 0.015.
Values may be sent and summed in bfloat16 or wider, within the bound.
A program may use at most 192 MiB of HBM per device.

v0:
```python
import math
import jax
import jax.numpy as jnp
from jax import lax
from jax.sharding import PartitionSpec as P

HEAD_DIM = 128
TOP = 6
PAGE = 16
epsilon = 1e-05
rope_base = 500000.0
masked_score = -1e30


def rms_norm(values, gain_vec):
    widened = values.astype(jnp.float32)
    factor = lax.rsqrt(jnp.mean(widened * widened, axis=-1, keepdims=True) + epsilon)
    return (widened * factor * gain_vec).astype(jnp.bfloat16)


def rotate(values, position):
    half_dim = values.shape[-1] // 2
    inverse = rope_base ** (-2.0 * jnp.arange(half_dim, dtype=jnp.float32) / values.shape[-1])
    angles = position.astype(jnp.float32)[:, None] * inverse[None, :]
    cosine = jnp.cos(angles)[:, None, :]
    sine_part = jnp.sin(angles)[:, None, :]
    first_half = values[..., :half_dim]
    second_half = values[..., half_dim:]
    return jnp.concatenate(
        [
            first_half * cosine - second_half * sine_part,
            second_half * cosine + first_half * sine_part,
        ],
        axis=-1,
    )


def segment_start(seg_lengths, positions):
    bounds = jnp.cumsum(seg_lengths)
    starts = bounds - seg_lengths
    return jnp.max(jnp.where(starts[None, :] <= positions[:, None], starts[None, :], 0), axis=1)


def over_blocks(step_fn, carried, portion, key_positions):
    rows = portion.shape[0]
    size = math.gcd(rows, 512)
    count = rows // size
    stacked = portion.reshape((count, size) + portion.shape[1:])
    pos_stack = key_positions.reshape(count, size)

    def turn(state, item):
        return (step_fn(state, item[0], item[1]), None)

    carried, unused = lax.scan(turn, carried, (stacked, pos_stack))
    return carried


def attend_piece(
    soft_state,
    queries,
    piece_keys,
    piece_values,
    key_positions,
    query_positions,
    query_first,
    scaling,
):
    running_max, row_total, accum_sum = soft_state
    scores = (
        jnp.einsum("qkgd,skd->qkgs", queries, piece_keys, preferred_element_type=jnp.float32)
        * scaling
    )
    allowed = (key_positions[None, :] <= query_positions[:, None]) & (
        key_positions[None, :] >= query_first[:, None]
    )
    allowed = allowed[:, None, None, :]
    scores = jnp.where(allowed, scores, masked_score)
    new_max = jnp.maximum(running_max, jnp.max(scores, axis=-1))
    weights = jnp.where(allowed, jnp.exp(scores - new_max[..., None]), 0.0)
    rescale = jnp.exp(running_max - new_max)
    row_total = row_total * rescale + jnp.sum(weights, axis=-1)
    product = jnp.einsum(
        "qkgs,skd->qkgd",
        weights.astype(jnp.bfloat16),
        piece_values,
        preferred_element_type=jnp.float32,
    )
    accum_sum = accum_sum * rescale[..., None] + product
    return (new_max, row_total, accum_sum)


def local(
    hidden,
    gain_attn,
    w_query,
    w_key,
    w_value,
    w_out,
    gain_moe,
    expert_ids,
    expert_gates,
    w_gate,
    w_up,
    w_down,
    seg_lengths,
    slot_page,
):
    tok_rows = hidden.shape[0]
    model_width = hidden.shape[1]
    shard_count = lax.axis_size("seq")
    shard_index = lax.axis_index("seq")
    tensor_index = lax.axis_index("tp")
    quarter = model_width // lax.axis_size("tp")
    kv_local = w_key.shape[1] // HEAD_DIM
    q_local = w_query.shape[1] // HEAD_DIM
    group_size = q_local // kv_local
    positions = shard_index * tok_rows + jnp.arange(tok_rows, dtype=jnp.int32)
    seg_first = segment_start(seg_lengths, positions)
    offsets = positions - seg_first
    normed = rms_norm(hidden, gain_attn)
    query_raw = jnp.dot(normed, w_query, preferred_element_type=jnp.float32).reshape(
        tok_rows, q_local, HEAD_DIM
    )
    queries = (
        rotate(query_raw, offsets)
        .astype(jnp.bfloat16)
        .reshape(tok_rows, kv_local, group_size, HEAD_DIM)
    )
    key_raw = jnp.dot(normed, w_key, preferred_element_type=jnp.float32).reshape(
        tok_rows, kv_local, HEAD_DIM
    )
    keys_rot = rotate(key_raw, offsets).astype(jnp.bfloat16)
    values = (
        jnp.dot(normed, w_value, preferred_element_type=jnp.float32)
        .astype(jnp.bfloat16)
        .reshape(tok_rows, kv_local, HEAD_DIM)
    )
    kv_rows = jnp.stack([keys_rot, values], axis=2)
    row_width = 2 * kv_local * HEAD_DIM
    slot_count = slot_page.shape[0] // shard_count
    own_slots = lax.dynamic_slice_in_dim(slot_page, shard_index * slot_count, slot_count)
    wanted = own_slots[:, None, None] * PAGE + jnp.arange(PAGE, dtype=jnp.int32)[None, :, None]
    scaling = HEAD_DIM ** (-0.5)
    empty_max = jnp.full((tok_rows, kv_local, group_size), masked_score, jnp.float32)
    empty_total = jnp.zeros((tok_rows, kv_local, group_size), jnp.float32)
    empty_sum = jnp.zeros((tok_rows, kv_local, group_size, HEAD_DIM), jnp.float32)
    empty_cache = jnp.zeros((slot_count, PAGE, row_width), jnp.float32)

    def cache_rows(cache_acc, portion, key_positions):
        piece_rows = portion.shape[0]
        chosen = (wanted == key_positions[None, None, :]).astype(jnp.bfloat16)
        return cache_acc + jnp.einsum(
            "spc,cw->spw",
            chosen,
            portion.reshape(piece_rows, row_width),
            preferred_element_type=jnp.float32,
        )

    def attend_rows(soft_state, portion, key_positions):
        return attend_piece(
            soft_state,
            queries,
            portion[:, :, 0],
            portion[:, :, 1],
            key_positions,
            positions,
            seg_first,
            scaling,
        )

    def both_rows(carried, portion, key_positions):
        soft_state, cache_acc = carried
        return (
            attend_rows(soft_state, portion, key_positions),
            cache_rows(cache_acc, portion, key_positions),
        )

    portion = lax.all_gather(kv_rows, "seq", axis=0, tiled=True)
    key_positions = jnp.arange(portion.shape[0], dtype=jnp.int32)
    soft_state, cache_acc = over_blocks(
        both_rows, ((empty_max, empty_total, empty_sum), empty_cache), portion, key_positions
    )
    running_max, row_total, accum_sum = soft_state
    attended = (
        (accum_sum / row_total[..., None])
        .astype(jnp.bfloat16)
        .reshape(tok_rows, q_local * HEAD_DIM)
    )
    kv_cache = cache_acc.astype(jnp.bfloat16)
    partial_value = jnp.dot(attended, w_out, preferred_element_type=jnp.float32)
    exp_local = w_gate.shape[0]
    experts_all = exp_local * shard_count
    capacity = (tok_rows * TOP * 3 // (2 * experts_all) + 7) // 8 * 8
    flat_ids = expert_ids.reshape(tok_rows * TOP)
    expert_hits = (flat_ids[:, None] == jnp.arange(experts_all, dtype=jnp.int32)[None, :]).astype(
        jnp.int32
    )
    slot_rank = jnp.sum((jnp.cumsum(expert_hits, axis=0) - 1) * expert_hits, axis=1)
    target = flat_ids * capacity + slot_rank
    places = (
        jnp.arange(experts_all * capacity, dtype=jnp.int32)[:, None, None]
        == target.reshape(tok_rows, TOP)[None, :, :]
    )
    selector = jnp.any(places, axis=2).astype(jnp.bfloat16)
    attn_full = lax.psum(partial_value.astype(jnp.bfloat16), "tp").astype(jnp.float32)
    mid = (hidden.astype(jnp.float32) + attn_full).astype(jnp.bfloat16)
    moe_in = rms_norm(mid, gain_moe)
    residual = lax.dynamic_slice_in_dim(mid, tensor_index * quarter, quarter, 1)
    packed = jnp.dot(selector, moe_in, preferred_element_type=jnp.float32).astype(jnp.bfloat16)
    rows_in = lax.all_to_all(
        packed.reshape(shard_count, exp_local, capacity, moe_in.shape[1]),
        "seq",
        split_axis=0,
        concat_axis=0,
        tiled=True,
    )
    gate_term = jnp.einsum("secd,edf->secf", rows_in, w_gate, preferred_element_type=jnp.float32)
    up_term = jnp.einsum("secd,edf->secf", rows_in, w_up, preferred_element_type=jnp.float32)
    hidden_act = (jax.nn.silu(gate_term) * up_term).astype(jnp.bfloat16)
    down_term = jnp.einsum("secf,efd->secd", hidden_act, w_down, preferred_element_type=jnp.float32)
    merged = lax.psum_scatter(down_term.astype(jnp.bfloat16), "tp", scatter_dimension=3, tiled=True)
    returned = lax.all_to_all(merged, "seq", split_axis=0, concat_axis=0, tiled=True)
    flat_back = returned.reshape(experts_all * capacity, quarter)
    picked = jnp.take(flat_back, target, axis=0).astype(jnp.float32).reshape(tok_rows, TOP, quarter)
    moe_out = jnp.einsum("tk,tkd->td", expert_gates, picked)
    final_rows = (residual.astype(jnp.float32) + moe_out).astype(jnp.bfloat16)
    return (final_rows, kv_cache)


def solution(mesh):
    placed = (
        P("seq", None),
        P(),
        P(None, "tp"),
        P(None, "tp"),
        P(None, "tp"),
        P("tp", None),
        P(),
        P("seq", None),
        P("seq", None),
        P("seq", None, "tp"),
        P("seq", None, "tp"),
        P("seq", "tp", None),
        P(),
        P(),
    )
    return jax.shard_map(
        local,
        mesh=mesh,
        in_specs=placed,
        out_specs=(P("seq", "tp"), P("seq", None, "tp")),
        check_vma=False,
    )
```

profile of v0, /device:TPU:1, one launch (start us, length us, event | category | flops | bytes accessed | tf_op | source)
XLA Modules:
  0.0 593.0 jit_solution(5520721394446283536)
XLA Ops:
  7.3 1.5 fusion.47
  11.5 1.7 fusion.55
  13.3 1.7 convolution_bitcast_fusion.1
  17.0 3.6 fusion.80
  23.4 41.2 %all-gather.2.cloned.1.call-done = bf16[4096,1,2,128]{0,3,2,1:T(8,128)(2,1)} async-done(((bf16[128,1,2,128]{0,3,2,1:T(8,128)(2,1)}), bf16[4096,1,2,128]{0,3,2,1:T(8,128)(2,1)}) %all-gather.2.cloned.1.call-update) | async-done | bytes 2097168 | tf_op jit(solution)/shard_map/all_gather | solution.py:178
  64.5 3.8 copy.103
  68.3 4.5 copy.78
  72.9 104.9 %while.17 = (s32[]{:T(128)}, f32[128,1,5]{0,2,1:T(8,128)S(1)}, f32[128,1,5]{0,2,1:T(8,128)S(1)}, f32[128,1,5,128]{0,3,2,1:T(8,128)}, f32[64,16,256]{2,1,0:T(8,12...) while((s32[]{:T(128)}, f32[128,1,5]{0,2,1:T(8,128)S(1)}, ...), condition=%wide.region_6.7_spmd.clone, body=%wide.region_3.6_spmd.clone.sunk | while | flops 440652672 | bytes 13333522 | solution.py:54
  74.9 1.4 compare_and_fusion.3
  79.2 1.8 reshape.490
  81.0 2.5 fusion.113
  87.7 1.4 compare_and_fusion.3
  92.0 1.8 reshape.490
  93.8 2.9 fusion.113
  100.9 1.4 compare_and_fusion.3
  105.1 1.8 reshape.490
  107.0 2.9 fusion.113
  114.0 1.4 compare_and_fusion.3
  118.3 1.8 reshape.490
  120.1 2.9 fusion.113
  131.4 1.8 reshape.490
  133.3 2.9 fusion.113
  144.6 1.8 reshape.490
  146.5 2.9 fusion.113
  157.8 1.8 reshape.490
  159.6 2.9 fusion.113
  170.9 1.8 reshape.490
  172.8 2.9 fusion.113
  178.8 1.6 convolution_convert_fusion.1
  180.6 1.8 reduce-window.20
  183.9 37.5 %all-reduce.2.cloned.1.call-done = bf16[128,2560]{1,0:T(8,128)(2,1)} async-done(((bf16[128,2560]{1,0:T(8,128)(2,1)}), bf16[128,2560]{1,0:T(8,128)(2,1)}) %all-reduce.2.cloned.1.call-update) | async-done | bytes 655376 | tf_op jit(solution)/shard_map/psum | solution.py:205
  221.4 1.4 fusion.44
  222.8 2.3 convolution_convert_fusion
  225.1 99.8 %all_to_all.10 = bf16[32,2,24,2560]{3,2,1,0:T(8,128)(2,1)S(1)} all-to-all(bf16[32,2,24,2560]{3,2,1,0:T(8,128)(2,1)S(1)} %bitcast.173), channel_id=1, replica_groups=mesh['seq'=32,'tp'=4] {'seq'}, dimensions={0} | all-to-all | bytes 15728640 | tf_op jit(solution)/shard_map/all_to_all | solution.py:210
  324.9 3.1 copy-done.6
  328.0 4.4 fusion.26
  332.4 13.8 %convert_bitcast_fusion = bf16[32,2,24,2560]{3,2,0,1:T(8,128)(2,1)} fusion(bf16[2,384,2560]{2,1,0:T(8,128)(2,1)} %param.27, f32[2,32,24,384]{3,2,1,0:T(8,128)S(1)} %fusion.26, bf16[2,2560,384]{2,1,0:T(8,128)(2,1)} %param.26, bf16[32,2,24,2560]{3,2,1,0:T(8,128)(2,1)} %copy-done.6), kind=kOutput, calls=%fused_computation.36 | convolution fusion | flops 6047268864 | bytes 25952256 | tf_op jit(solution)/shard_map/secf,efd->secd/dot_general | solution.py:220
  346.2 35.5 %copy.99 = bf16[32,2,24,2560]{2,0,1,3:T(8,128)(2,1)} copy(bf16[32,2,24,2560]{3,2,0,1:T(8,128)(2,1)} %convert_bitcast_fusion) | data formatting | bytes 15728640
  381.7 57.5 %reshape.481 = bf16[2560,1536]{1,0:T(8,128)(2,1)} reshape(bf16[2560,2,32,24]{3,2,1,0:T(8,128)(2,1)} %bitcast.172) | data formatting | bytes 15728640
  439.3 73.7 %reduce-scatter.4.cloned.1.call-done = bf16[640,1536]{1,0:T(8,128)(2,1)} async-done(((bf16[2560,1536]{1,0:T(8,128)(2,1)}), bf16[640,1536]{1,0:T(8,128)(2,1)}) %reduce-scatter.4.cloned.1.call-update) | async-done | bytes 1966096
  513.0 18.8 %reshape.482 = bf16[640,2,32,24]{3,2,1,0:T(8,128)(2,1)} reshape(bf16[640,1536]{1,0:T(8,128)(2,1)} %reduce-scatter.4.cloned.1.call-done) | data formatting | bytes 3932160
  531.9 10.0 %copy.87 = bf16[32,2,24,640]{3,2,1,0:T(8,128)(2,1)} copy(bf16[32,2,24,640]{2,0,1,3:T(8,128)(2,1)} %bitcast.175) | data formatting | bytes 3932160 | tf_op jit(solution)/shard_map/reduce_scatter | solution.py:221
  541.9 7.7 %all-to-all-start.1 = ((bf16[32,2,24,640]{3,2,1,0:T(8,128)(2,1)}), bf16[32,2,24,640]{3,2,1,0:T(8,128)(2,1)S(1)}, u32[]{:S(2)}, u32[]{:S(2)}) async-start(bf16[32,2,24,640]{3,2,1,0:T(8,128)(2,1)} %copy.87), calls=%async_computation.1 | async-start | bytes 3932160 | tf_op jit(solution)/shard_map/all_to_all | solution.py:222
  551.1 25.4 %all-to-all-done.1 = bf16[32,2,24,640]{3,2,1,0:T(8,128)(2,1)S(1)} async-done(((bf16[32,2,24,640]{3,2,1,0:T(8,128)(2,1)}), bf16[32,2,24,640]{3,2,1,0:T(8,128)(2,1)S(1)}, u32[]{:S(2)}, u32[]{:S(2)}) %all-to-all-start.1) | async-done | bytes 1966112 | tf_op jit(solution)/shard_map/all_to_all | solution.py:222
  576.5 3.4 gather_fusion
  580.0 2.9 gather.7
  582.9 1.9 fusion.51
  584.8 1.6 fusion.60
  (239 shorter events, 73.2 us)
Async XLA Ops:
  7.2 171.6 %copy-start = (bf16[640,2560]{1,0:T(8,128)(2,1)S(1)}, bf16[640,2560]{1,0:T(8,128)(2,1)}, u32[]{:S(2)}) copy-start(bf16[640,2560]{1,0:T(8,128)(2,1)} %param.21) | copy-start | bytes 9830404
  7.2 6.1 %copy-start.14 = (f32[2560]{0:T(1024)S(1)}, f32[2560]{0:T(1024)}, u32[]{:S(2)}) copy-start(f32[2560]{0:T(1024)} %param.17) | copy-start | bytes 30724
  7.2 8.8 %copy-start.12 = (s32[128,6]{0,1:T(8,128)S(1)}, s32[128,6]{0,1:T(8,128)}, u32[]{:S(2)}) copy-start(s32[128,6]{0,1:T(8,128)} %param.23) | copy-start | bytes 9220
  7.2 57.3 %all-gather.2.cloned.1.call-start = ((), (), s32[]{:S(2)}) async-start(), calls=%async_computation.3 | async-start | bytes 2162688 | tf_op jit(solution)/shard_map/all_gather | solution.py:178
  15.9 205.5 %all-reduce.2.cloned.1.call-start = ((), (), s32[]{:S(2)}) async-start(), calls=%async_computation.4 | async-start | bytes 1310720 | tf_op jit(solution)/shard_map/psum | solution.py:205
  16.1 4.5 copy-start.10
  81.0 2.5 copy-start.3
  81.0 2.5 copy-start.7
  83.6 1.0 copy-start.4
  84.9 0.7 copy-start.5
  93.8 2.9 copy-start.3
  93.8 2.9 copy-start.7
  96.7 1.0 copy-start.4
  98.1 0.7 copy-start.5
  107.0 2.9 copy-start.3
  107.0 2.9 copy-start.7
  109.9 1.0 copy-start.4
  111.3 0.7 copy-start.5
  120.1 2.9 copy-start.3
  120.1 2.9 copy-start.7
  123.0 1.0 copy-start.4
  124.4 0.7 copy-start.5
  133.3 2.9 copy-start.3
  133.3 2.9 copy-start.7
  136.2 1.0 copy-start.4
  137.6 0.7 copy-start.5
  146.4 2.9 copy-start.3
  146.4 2.9 copy-start.7
  149.4 1.0 copy-start.4
  150.7 0.7 copy-start.5
  159.6 2.9 copy-start.3
  159.6 2.9 copy-start.7
  162.5 1.0 copy-start.4
  172.8 2.9 copy-start.3
  172.8 2.9 copy-start.7
  175.7 1.0 copy-start.4
  178.8 1.7 copy-start.13
  178.8 1.7 copy-start.11
  180.4 41.0 %copy-start.8 = (bf16[128,2560]{1,0:T(8,128)(2,1)S(1)}, bf16[128,2560]{1,0:T(8,128)(2,1)}, u32[]{:S(2)}) copy-start(bf16[128,2560]{1,0:T(8,128)(2,1)} %param.16) | copy-start | bytes 1966084
  180.4 42.4 %copy-start.15 = (f32[2560]{0:T(1024)S(1)}, f32[2560]{0:T(1024)}, u32[]{:S(2)}) copy-start(f32[2560]{0:T(1024)} %param.22) | copy-start | bytes 30724
  180.4 332.6 %reduce-scatter.4.cloned.1.call-start = ((), (), s32[]{:S(2)}) async-start(), calls=%async_computation.5 | async-start | bytes 9830400
  222.8 2.3 copy-start.9
  225.1 102.8 %copy-start.17 = (bf16[2,2560,384]{2,1,0:T(8,128)(2,1)S(1)}, bf16[2,2560,384]{2,1,0:T(8,128)(2,1)}, u32[]{:S(2)}) copy-start(bf16[2,2560,384]{2,1,0:T(8,128)(2,1)} %param.25) | copy-start | bytes 11796484
  324.9 3.1 copy-start.6
  541.9 8.0 %copy-start.16 = (f32[128,6]{0,1:T(8,128)S(1)}, f32[128,6]{0,1:T(8,128)}, u32[]{:S(2)}) copy-start(f32[128,6]{0,1:T(8,128)} %param.24) | copy-start | bytes 9220
  541.9 8.4 %copy-start.2 = (f32[64,16,256]{2,1,0:T(8,128)S(1)}, f32[64,16,256]{2,1,0:T(8,128)}, u32[]{:S(2)}) copy-start(f32[64,16,256]{2,1,0:T(8,128)} %get-tuple-element.63) | copy-start | bytes 3145732
  541.9 34.6 %all-to-all-start.1 = ((bf16[32,2,24,640]{3,2,1,0:T(8,128)(2,1)}), bf16[32,2,24,640]{3,2,1,0:T(8,128)(2,1)S(1)}, u32[]{:S(2)}, u32[]{:S(2)}) async-start(bf16[32,2,24,640]{3,2,1,0:T(8,128)(2,1)} %copy.87), calls=%async_computation.1 | async-start | bytes 3932160 | tf_op jit(solution)/shard_map/all_to_all | solution.py:222
  580.0 6.5 %copy-start.1 = (bf16[640,2560]{1,0:T(8,128)(2,1)S(1)}, bf16[640,2560]{1,0:T(8,128)(2,1)}, u32[]{:S(2)}) copy-start(bf16[640,2560]{1,0:T(8,128)(2,1)} %param.21) | copy-start | bytes 9830404
  (2 other events, 1.5 us)
Sparse Core Ops, SparseCore 0:
  16.0 48.5 all-gather.1
  180.5 40.8 all-reduce.1
  439.4 73.5 reduce-scatter.3
where the time goes:
time: 598 us; the launch traced here: 593 us
  local copies, waits for them, and re-layouts  195 us (33%)
  waiting for transfers between devices  178 us (30%)
  blocking collectives  99.8 us (17%)
  matrix products  59.8 us (10%)
  other arithmetic  37.6 us (6%)
  between operations  14.1 us (2%)
  starting transfers between devices  7.86 us (1%)
    unnamed x36, local copies, waits for them, and re-layouts  124 us
    all_to_all x1, blocking collectives, local(): lax.all_to_all(packed.reshape(shard_count, exp_local, capacity, moe_in.sh...  99.8 us
    unnamed x4, waiting for transfers between devices  73.8 us
    all_gather x1, waiting for transfers between devices, local(): portion = lax.all_gather(kv_rows, 'seq', axis=0, tiled=True)  41.2 us
    psum x1, waiting for transfers between devices, local(): lax.psum(partial_value.astype(jnp.bfloat16), 'tp').astype(jnp.float32)  37.5 us
    all_to_all x1, waiting for transfers between devices, local(): lax.all_to_all(merged, 'seq', split_axis=0, concat_axis=0, tiled=True)  25.4 us
    dot_general x8, matrix products, cache_rows(): jnp.einsum('spc,cw->spw', chosen, portion.reshape(piece_rows, row_width),...  22.8 us
    dynamic_slice x24, local copies, waits for them, and re-layouts, over_blocks(): carried, unused = lax.scan(turn, carried, (stacked, pos_stack))  21.4 us
  transfers between devices with their start and end apart: 4, of which 4 were waited for; matrix products, arithmetic and copies ran while one was open for 2% of the time, Pallas kernels for 0%

commit v1 on v0

--- a/solution.py
+++ b/solution.py
@@ -175,7 +175,19 @@
             cache_rows(cache_acc, portion, key_positions),
         )
 
-    portion = lax.all_gather(kv_rows, "seq", axis=0, tiled=True)
+    def _handle_wall(v0):
+        part_next = jnp.concatenate(
+            jax.lax.all_to_all(
+                jnp.stack([v0] * jax.lax.axis_size("seq"), 0),
+                axis_name="seq",
+                split_axis=0,
+                concat_axis=0,
+            ),
+            0,
+        )
+        return part_next
+
+    portion = _handle_wall(kv_rows)
     key_positions = jnp.arange(portion.shape[0], dtype=jnp.int32)
     soft_state, cache_acc = over_blocks(
         both_rows, ((empty_max, empty_total, empty_sum), empty_cache), portion, key_positions

time: 598 us -> 557 us (0.931)
  waiting for transfers between devices: 178 us -> 157 us
  local copies, waits for them, and re-layouts: 195 us -> 179 us
  other arithmetic: 37.6 us -> 24.9 us
  starting transfers between devices: 7.86 us -> 17.4 us
    all_gather x1 -> x0, waiting for transfers between devices: 41.2 us -> none  [local(): portion = lax.all_gather(kv_rows, 'seq', axis=0, tiled=True)]
    all_to_all x0 -> x1, waiting for transfers between devices: none -> 22 us  [_handle_wall(): jax.lax.all_to_all(jnp.stack([v0] * jax.lax.axis_size('seq'), 0), axis_na...]
    all_to_all x0 -> x1, starting transfers between devices: none -> 9.61 us  [_handle_wall(): jax.lax.all_to_all(jnp.stack([v0] * jax.lax.axis_size('seq'), 0), axis_na...]
    unnamed x36 -> x34, local copies, waits for them, and re-layouts: 124 us -> 116 us
    squeeze x8 -> x0, local copies, waits for them, and re-layouts: 7.74 us -> none  [over_blocks(): carried, unused = lax.scan(turn, carried, (stacked, pos_stack))]
    unnamed x4 -> x3, waiting for transfers between devices: 73.8 us -> 73.8 us
where the time goes in v1:
time: 557 us; the launch traced here: 554 us
  local copies, waits for them, and re-layouts  179 us (32%)
  waiting for transfers between devices  157 us (28%)
  blocking collectives  99.8 us (18%)
  matrix products  59.2 us (11%)
  other arithmetic  24.9 us (4%)
  starting transfers between devices  17.4 us (3%)
  between operations  14.4 us (3%)
    unnamed x34, local copies, waits for them, and re-layouts  116 us
    all_to_all x1, blocking collectives, local(): lax.all_to_all(packed.reshape(shard_count, exp_local, capacity, moe_in.sh...  99.8 us
    unnamed x3, waiting for transfers between devices  73.8 us
    psum x1, waiting for transfers between devices, local(): lax.psum(partial_value.astype(jnp.bfloat16), 'tp').astype(jnp.float32)  36.2 us
    all_to_all x1, waiting for transfers between devices, local(): lax.all_to_all(merged, 'seq', split_axis=0, concat_axis=0, tiled=True)  25.4 us
    dot_general x8, matrix products, cache_rows(): jnp.einsum('spc,cw->spw', chosen, portion.reshape(piece_rows, row_width),...  22.2 us
    all_to_all x1, waiting for transfers between devices, _handle_wall(): jax.lax.all_to_all(jnp.stack([v0] * jax.lax.axis_size('seq'), 0), axis_na...  22 us
    dynamic_slice x24, local copies, waits for them, and re-layouts, over_blocks(): carried, unused = lax.scan(turn, carried, (stacked, pos_stack))  21.8 us
  transfers between devices with their start and end apart: 4, of which 4 were waited for; matrix products, arithmetic and copies ran while one was open for 2% of the time, Pallas kernels for 0%

profile of v1, /device:TPU:1, one launch (start us, length us, event | category | flops | bytes accessed | tf_op | source)
XLA Modules:
  0.0 553.5 jit_solution(6956202927745606)
XLA Ops:
  7.2 1.5 fusion.47
  10.3 1.7 fusion.55
  12.1 1.7 convolution_bitcast_fusion.1
  14.2 1.9 stack.8
  16.1 9.6 %all-to-all-start = ((bf16[32,128,1,2,128]{4,1,3,2,0:T(8,128)(2,1)}), bf16[32,128,1,2,128]{4,1,3,2,0:T(8,128)(2,1)}, u32[]{:S(2)}, u32[]{:S(2)}) async-start(bf16[32,128,1,2,128]{4,1,3,2,0:T(8,128)(2,1)} %stack.8), calls=%async_computation | async-start | bytes 4194304 | tf_op jit(solution)/shard_map/all_to_all | solution.py:180
  26.8 3.6 fusion.80
  32.0 22.0 %all-to-all-done = bf16[32,128,1,2,128]{4,1,3,2,0:T(8,128)(2,1)} async-done(((bf16[32,128,1,2,128]{4,1,3,2,0:T(8,128)(2,1)}), bf16[32,128,1,2,128]{4,1,3,2,0:T(8,128)(2,1)}, u32[]{:S(2)}, u32[]{:S(2)}) %all-to-all-start) | async-done | bytes 2097184 | tf_op jit(solution)/shard_map/all_to_all | solution.py:180
  54.0 3.2 copy.83
  57.2 82.0 %while.17 = (s32[]{:T(128)}, f32[128,1,5]{0,2,1:T(8,128)S(1)}, f32[128,1,5]{0,2,1:T(8,128)S(1)}, f32[128,1,5,128]{0,3,2,1:T(8,128)}, f32[64,16,256]{2,1,0:T(8,12...) while((s32[]{:T(128)}, f32[128,1,5]{0,2,1:T(8,128)S(1)}, ...), condition=%wide.region_6.7_spmd.clone, body=%wide.region_3.6_spmd.clone.sunk | while | flops 440652672 | bytes 14257362 | solution.py:54
  58.7 1.7 dynamic-slice_bitcast_fusion.3
  62.5 2.3 fusion.110
  68.5 1.7 dynamic-slice_bitcast_fusion.3
  72.4 2.8 fusion.110
  78.8 1.7 dynamic-slice_bitcast_fusion.3
  82.7 2.8 fusion.110
  89.1 1.7 dynamic-slice_bitcast_fusion.3
  91.9 1.1 reshape.489
  93.0 2.8 fusion.110
  99.5 1.7 dynamic-slice_bitcast_fusion.3
  102.2 1.1 reshape.489
  103.3 2.8 fusion.110
  109.8 1.7 dynamic-slice_bitcast_fusion.3
  112.5 1.1 reshape.489
  113.7 2.8 fusion.110
  120.1 1.7 dynamic-slice_bitcast_fusion.3
  124.0 2.8 fusion.110
  130.4 1.7 dynamic-slice_bitcast_fusion.3
  134.3 2.8 fusion.110
  140.3 1.6 convolution_convert_fusion.1
  142.1 1.8 reduce-window.20
  145.4 36.2 %all-reduce.2.cloned.1.call-done = bf16[128,2560]{1,0:T(8,128)(2,1)} async-done(((bf16[128,2560]{1,0:T(8,128)(2,1)}), bf16[128,2560]{1,0:T(8,128)(2,1)}) %all-reduce.2.cloned.1.call-update) | async-done | bytes 655376 | tf_op jit(solution)/shard_map/psum | solution.py:217
  181.6 1.4 fusion.44
  183.0 2.3 convolution_convert_fusion
  185.3 99.8 %all_to_all.15 = bf16[32,2,24,2560]{3,2,1,0:T(8,128)(2,1)S(1)} all-to-all(bf16[32,2,24,2560]{3,2,1,0:T(8,128)(2,1)S(1)} %bitcast.172), channel_id=1, replica_groups=mesh['seq'=32,'tp'=4] {'seq'}, dimensions={0} | all-to-all | bytes 15728640 | tf_op jit(solution)/shard_map/all_to_all | solution.py:222
  285.1 3.1 copy-done.7
  288.2 4.4 fusion.26
  292.6 13.8 %convert_bitcast_fusion = bf16[32,2,24,2560]{3,2,0,1:T(8,128)(2,1)} fusion(bf16[2,384,2560]{2,1,0:T(8,128)(2,1)} %param.27, f32[2,32,24,384]{3,2,1,0:T(8,128)S(1)} %fusion.26, bf16[2,2560,384]{2,1,0:T(8,128)(2,1)} %param.26, bf16[32,2,24,2560]{3,2,1,0:T(8,128)(2,1)} %copy-done.7), kind=kOutput, calls=%fused_computation.37 | convolution fusion | flops 6047268864 | bytes 25952256 | tf_op jit(solution)/shard_map/secf,efd->secd/dot_general | solution.py:232
  306.4 35.5 %copy.106 = bf16[32,2,24,2560]{2,0,1,3:T(8,128)(2,1)} copy(bf16[32,2,24,2560]{3,2,0,1:T(8,128)(2,1)} %convert_bitcast_fusion) | data formatting | bytes 15728640
  342.0 57.5 %reshape.480 = bf16[2560,1536]{1,0:T(8,128)(2,1)} reshape(bf16[2560,2,32,24]{3,2,1,0:T(8,128)(2,1)} %bitcast.171) | data formatting | bytes 15728640
  399.5 73.7 %reduce-scatter.4.cloned.1.call-done = bf16[640,1536]{1,0:T(8,128)(2,1)} async-done(((bf16[2560,1536]{1,0:T(8,128)(2,1)}), bf16[640,1536]{1,0:T(8,128)(2,1)}) %reduce-scatter.4.cloned.1.call-update) | async-done | bytes 1966096
  473.2 18.8 %reshape.481 = bf16[640,2,32,24]{3,2,1,0:T(8,128)(2,1)} reshape(bf16[640,1536]{1,0:T(8,128)(2,1)} %reduce-scatter.4.cloned.1.call-done) | data formatting | bytes 3932160
  492.1 10.0 %copy.94 = bf16[32,2,24,640]{3,2,1,0:T(8,128)(2,1)} copy(bf16[32,2,24,640]{2,0,1,3:T(8,128)(2,1)} %bitcast.174) | data formatting | bytes 3932160 | tf_op jit(solution)/shard_map/reduce_scatter | solution.py:233
  502.1 7.7 %all-to-all-start.2 = ((bf16[32,2,24,640]{3,2,1,0:T(8,128)(2,1)}), bf16[32,2,24,640]{3,2,1,0:T(8,128)(2,1)S(1)}, u32[]{:S(2)}, u32[]{:S(2)}) async-start(bf16[32,2,24,640]{3,2,1,0:T(8,128)(2,1)} %copy.94), calls=%async_computation.2 | async-start | bytes 3932160 | tf_op jit(solution)/shard_map/all_to_all | solution.py:234
  511.4 25.4 %all-to-all-done.2 = bf16[32,2,24,640]{3,2,1,0:T(8,128)(2,1)S(1)} async-done(((bf16[32,2,24,640]{3,2,1,0:T(8,128)(2,1)}), bf16[32,2,24,640]{3,2,1,0:T(8,128)(2,1)S(1)}, u32[]{:S(2)}, u32[]{:S(2)}) %all-to-all-start.2) | async-done | bytes 1966112 | tf_op jit(solution)/shard_map/all_to_all | solution.py:234
  536.8 3.4 gather_fusion
  540.2 2.9 gather.7
  543.1 1.9 fusion.51
  545.0 1.6 fusion.60
  (343 shorter events, 50.2 us)
Async XLA Ops:
  7.2 133.1 %copy-start = (bf16[640,2560]{1,0:T(8,128)(2,1)S(1)}, bf16[640,2560]{1,0:T(8,128)(2,1)}, u32[]{:S(2)}) copy-start(bf16[640,2560]{1,0:T(8,128)(2,1)} %param.21) | copy-start | bytes 9830404
  7.2 4.9 copy-start.21
  16.1 9.7 %copy-start.15 = (s32[128,6]{0,1:T(8,128)S(1)}, s32[128,6]{0,1:T(8,128)}, u32[]{:S(2)}) copy-start(s32[128,6]{0,1:T(8,128)} %param.23) | copy-start | bytes 9220
  16.1 38.0 %all-to-all-start = ((bf16[32,128,1,2,128]{4,1,3,2,0:T(8,128)(2,1)}), bf16[32,128,1,2,128]{4,1,3,2,0:T(8,128)(2,1)}, u32[]{:S(2)}, u32[]{:S(2)}) async-start(bf16[32,128,1,2,128]{4,1,3,2,0:T(8,128)(2,1)} %stack.8), calls=%async_computation | async-start | bytes 4194304 | tf_op jit(solution)/shard_map/all_to_all | solution.py:180
  25.7 155.9 %all-reduce.2.cloned.1.call-start = ((), (), s32[]{:S(2)}) async-start(), calls=%async_computation.4 | async-start | bytes 1310720 | tf_op jit(solution)/shard_map/psum | solution.py:217
  25.9 4.5 copy-start.11
  57.2 3.2 copy-start.13
  57.2 3.2 copy-start.17
  57.2 3.2 copy-start.19
  67.0 3.2 copy-start.13
  67.0 3.2 copy-start.17
  67.0 3.2 copy-start.19
  72.4 2.9 copy-start.3
  72.4 2.9 copy-start.4
  77.3 3.2 copy-start.13
  77.3 3.2 copy-start.17
  77.4 3.2 copy-start.19
  82.7 2.9 copy-start.3
  87.7 3.2 copy-start.13
  87.7 3.2 copy-start.17
  87.7 3.2 copy-start.19
  93.0 2.9 copy-start.3
  93.0 2.9 copy-start.4
  98.0 3.2 copy-start.13
  98.0 3.2 copy-start.17
  98.0 3.2 copy-start.19
  103.3 2.9 copy-start.3
  108.3 3.2 copy-start.13
  108.3 3.2 copy-start.17
  108.3 3.2 copy-start.19
  113.6 2.9 copy-start.3
  118.6 3.2 copy-start.13
  118.6 3.2 copy-start.17
  118.6 3.2 copy-start.19
  124.0 2.9 copy-start.3
  128.9 3.2 copy-start.13
  128.9 3.2 copy-start.17
  129.0 3.2 copy-start.19
  134.3 2.9 copy-start.3
  141.9 39.7 %copy-start.9 = (bf16[128,2560]{1,0:T(8,128)(2,1)S(1)}, bf16[128,2560]{1,0:T(8,128)(2,1)}, u32[]{:S(2)}) copy-start(bf16[128,2560]{1,0:T(8,128)(2,1)} %param.16) | copy-start | bytes 1966084
  141.9 41.2 %copy-start.22 = (f32[2560]{0:T(1024)S(1)}, f32[2560]{0:T(1024)}, u32[]{:S(2)}) copy-start(f32[2560]{0:T(1024)} %param.22) | copy-start | bytes 30724
  141.9 331.4 %reduce-scatter.4.cloned.1.call-start = ((), (), s32[]{:S(2)}) async-start(), calls=%async_computation.5 | async-start | bytes 9830400
  185.3 102.8 %copy-start.24 = (bf16[2,2560,384]{2,1,0:T(8,128)(2,1)S(1)}, bf16[2,2560,384]{2,1,0:T(8,128)(2,1)}, u32[]{:S(2)}) copy-start(bf16[2,2560,384]{2,1,0:T(8,128)(2,1)} %param.25) | copy-start | bytes 11796484
  285.1 3.1 copy-start.7
  502.1 8.0 %copy-start.23 = (f32[128,6]{0,1:T(8,128)S(1)}, f32[128,6]{0,1:T(8,128)}, u32[]{:S(2)}) copy-start(f32[128,6]{0,1:T(8,128)} %param.24) | copy-start | bytes 9220
  502.1 8.4 %copy-start.2 = (f32[64,16,256]{2,1,0:T(8,128)S(1)}, f32[64,16,256]{2,1,0:T(8,128)}, u32[]{:S(2)}) copy-start(f32[64,16,256]{2,1,0:T(8,128)} %get-tuple-element.63) | copy-start | bytes 3145732
  502.1 34.6 %all-to-all-start.2 = ((bf16[32,2,24,640]{3,2,1,0:T(8,128)(2,1)}), bf16[32,2,24,640]{3,2,1,0:T(8,128)(2,1)S(1)}, u32[]{:S(2)}, u32[]{:S(2)}) async-start(bf16[32,2,24,640]{3,2,1,0:T(8,128)(2,1)} %copy.94), calls=%async_computation.2 | async-start | bytes 3932160 | tf_op jit(solution)/shard_map/all_to_all | solution.py:234
  540.2 6.5 %copy-start.1 = (bf16[640,2560]{1,0:T(8,128)(2,1)S(1)}, bf16[640,2560]{1,0:T(8,128)(2,1)}, u32[]{:S(2)}) copy-start(bf16[640,2560]{1,0:T(8,128)(2,1)} %param.21) | copy-start | bytes 9830404
  (58 other events, 102.1 us)
Sparse Core Ops, SparseCore 0:
  142.0 39.5 all-reduce.1
  399.6 73.5 reduce-scatter.3
